TPU v7x, 32 devices: a whole 2x2x4 slice. The times are simulated.
32 devices in a mesh: reach: 2 (over y), row: 4 (over z), col: 4 (over x, core).
Axes of the slice: x: 2, y: 2, z: 4, core: 2. Of those that a mesh axis runs over, the one named last changes fastest.
Arguments:
- operator: float32 [2048, 65536], P(('reach', 'col'), 'row'), parts along dimension 0, may hold values from -0.03125 to 0.03125
- basis: float32 [131072, 256], P(('reach', 'row')), parts along dimension 0, may hold values from -6 to 6
Outputs:
- image: float32 [2048, 256], P(('reach', 'row')), parts along dimension 0
There are 2 independent parts, one for each index of `reach`. A program takes and returns all parts, laid end to end along the dimension named above; each array names one. Nothing has to cross between parts.
All inputs are finite; a program needn't handle non-finite values.
Results may differ from a plain program's by a relative error of at most 0.000071.
Values sent between devices are 32-bit elements; how exact they have to be, the bound alone decides.
No kernel may reach another device: no remote copies, remote signals or barrier semaphores. Data moves between devices by JAX's collectives and lax.ppermute only.
A program may use at most 64 MiB of HBM per device.

v0:
```python
import jax
import jax.numpy as jnp
from jax import lax
from jax.sharding import PartitionSpec as P


def spread(value, axis, source):
    kept = jnp.where(lax.axis_index(axis) == source, value, 0).astype(value.dtype)
    return lax.psum(kept, axis)


def shards(operator, basis):
    partial_sum = jnp.dot(
        operator, basis, preferred_element_type=jnp.float32, precision=lax.Precision.HIGHEST
    )
    tile_rows = operator.shape[0]
    n_row = lax.axis_size("row")
    n_col = lax.axis_size("col")
    group = n_row // n_col
    out_rows = tile_rows * n_col // n_row
    summed = lax.psum(partial_sum, "row")
    row_index = lax.axis_index("row")
    offset = row_index % group * out_rows
    picked = lax.dynamic_slice_in_dim(summed, offset, out_rows, 0)
    return spread(picked, "col", row_index // group)


def solution(mesh):
    in_specs = (P(("reach", "col"), "row"), P(("reach", "row"), None))
    out_specs = P(("reach", "row"), None)
    return jax.shard_map(shards, mesh=mesh, in_specs=in_specs, out_specs=out_specs, check_vma=False)
```

profile of v0, /device:TPU:0, one launch (start us, length us, event | category | flops | bytes accessed | tf_op | source)
XLA Modules:
  0.0 106.0 jit_solution(11191584294463896214)
XLA Ops:
  6.5 0.0 all-reduce.3.cloned.1.call-start
  6.5 18.6 %fusion = f32[256,256]{1,0:T(8,128)} fusion(f32[256,16384]{1,0:T(8,128)} %param.2, f32[16384,256]{1,0:T(8,128)} %param.3), kind=kOutput, calls=%fused_computation.1 | convolution fusion | flops 12884901888 | bytes 33816576 | tf_op jit(solution)/shard_map/dot_general | solution.py:13
  25.2 0.0 all-reduce.3.cloned.1.call-update
  25.2 0.0 all-reduce.5.cloned.1.call-start
  25.2 38.1 %all-reduce.3.cloned.1.call-done = f32[256,256]{1,0:T(8,128)} async-done(((f32[256,256]{1,0:T(8,128)}), f32[256,256]{1,0:T(8,128)}) %all-reduce.3.cloned.1.call-update) | async-done | bytes 262160 | tf_op jit(solution)/shard_map/psum | solution.py:21
  63.3 1.7 %broadcast_select_fusion = f32[256,256]{1,0:T(8,128)} fusion(f32[256,256]{1,0:T(8,128)} %all-reduce.3.cloned.1.call-done, pred[]{:T(512)S(6)} %eq.5), kind=kLoop, calls=%fused_computation | loop fusion | flops 65536 | bytes 524289 | tf_op jit(solution)/shard_map/jit(_where)/select_n | solution.py:8
  65.0 0.0 all-reduce.5.cloned.1.call-update
  65.0 32.5 %all-reduce.5.cloned.1.call-done = f32[256,256]{1,0:T(8,128)} async-done(((f32[256,256]{1,0:T(8,128)}), f32[256,256]{1,0:T(8,128)}) %all-reduce.5.cloned.1.call-update) | async-done | bytes 262160 | tf_op jit(solution)/shard_map/psum | solution.py:9
  97.5 1.7 %copy.5 = f32[256,256]{1,0:T(8,128)} copy(f32[256,256]{1,0:T(8,128)} %all-reduce.5.cloned.1.call-done) | data formatting | bytes 524288
Async XLA Ops:
  6.5 56.8 %all-reduce.3.cloned.1.call-start = ((), (), s32[]{:S(2)}) async-start(), calls=%async_computation | async-start | bytes 524288 | tf_op jit(solution)/shard_map/psum | solution.py:21
  25.2 72.3 %all-reduce.5.cloned.1.call-start = ((), (), s32[]{:S(2)}) async-start(), calls=%async_computation.1 | async-start | bytes 524288 | tf_op jit(solution)/shard_map/psum | solution.py:9
Sparse Core Ops, SparseCore 0:
  25.3 37.9 all-reduce.2
  65.8 31.6 all-reduce.4
where the time goes:
time: 106 us
  waiting for transfers between devices  70.6 us (67%)
  matrix products  18.6 us (18%)
  between operations  13.4 us (13%)
  other arithmetic  1.67 us (2%)
  local copies, waits for them, and re-layouts  1.67 us (2%)
    psum x1, waiting for transfers between devices, shards(): summed = lax.psum(partial_sum, 'row')  38.1 us
    psum x1, waiting for transfers between devices, spread(): return lax.psum(kept, axis)  32.5 us
    dot_general x1, matrix products, shards(): jnp.dot(operator, basis, preferred_element_type=jnp.float32, precision=la...  18.6 us
  transfers between devices with their start and end apart: 2, of which 2 were waited for; matrix products, arithmetic and copies ran while one was open for 0% of the time, Pallas kernels for 0%

commit v1 on v0

--- a/solution.py
+++ b/solution.py
@@ -2,6 +2,7 @@
 import jax.numpy as jnp
 from jax import lax
 from jax.sharding import PartitionSpec as P
+from jax.lax import all_gather
 
 
 def spread(value, axis, source):
@@ -10,6 +11,11 @@
 
 
 def shards(operator, basis):
+
+    def link_block(point, group_axis):
+        outer = all_gather(point, group_axis).sum(axis=0)
+        return outer
+
     partial_sum = jnp.dot(
         operator, basis, preferred_element_type=jnp.float32, precision=lax.Precision.HIGHEST
     )
@@ -18,7 +24,7 @@
     n_col = lax.axis_size("col")
     group = n_row // n_col
     out_rows = tile_rows * n_col // n_row
-    summed = lax.psum(partial_sum, "row")
+    summed = link_block(partial_sum, "row")
     row_index = lax.axis_index("row")
     offset = row_index % group * out_rows
     picked = lax.dynamic_slice_in_dim(summed, offset, out_rows, 0)

time: 106 us -> 98.5 us (0.929)
  waiting for transfers between devices: 70.6 us -> 62.5 us
    psum x1 -> x0, waiting for transfers between devices: 38.1 us -> none  [shards(): summed = lax.psum(partial_sum, 'row')]
    all_gather x0 -> x1, waiting for transfers between devices: none -> 30.7 us  [link_block(): outer = all_gather(point, group_axis).sum(axis=0)]
    reduce_sum x0 -> x1, other arithmetic: none -> 1.32 us  [link_block(): outer = all_gather(point, group_axis).sum(axis=0)]
where the time goes in v1:
time: 98.5 us; the launch traced here: 98.3 us
  waiting for transfers between devices  62.5 us (63%)
  matrix products  18.6 us (19%)
  between operations  13.4 us (14%)
  other arithmetic  2.05 us (2%)
  local copies, waits for them, and re-layouts  1.67 us (2%)
    psum x1, waiting for transfers between devices, spread(): return lax.psum(kept, axis)  31.8 us
    all_gather x1, waiting for transfers between devices, link_block(): outer = all_gather(point, group_axis).sum(axis=0)  30.7 us
    dot_general x1, matrix products, shards(): jnp.dot(operator, basis, preferred_element_type=jnp.float32, precision=la...  18.6 us
  transfers between devices with their start and end apart: 2, of which 2 were waited for; matrix products, arithmetic and copies ran while one was open for 0% of the time, Pallas kernels for 0%

profile of v1, /device:TPU:0, one launch (start us, length us, event | category | flops | bytes accessed | tf_op | source)
XLA Modules:
  0.0 98.3 jit_solution(8070072653539677769)
XLA Ops:
  6.5 0.0 all-gather.3.cloned.1.call-start
  6.5 18.6 %fusion = f32[256,256]{1,0:T(8,128)} fusion(f32[256,16384]{1,0:T(8,128)} %param.2, f32[16384,256]{1,0:T(8,128)} %param.3), kind=kOutput, calls=%fused_computation.1 | convolution fusion | flops 12884901888 | bytes 33816576 | tf_op jit(solution)/shard_map/dot_general | solution.py:19
  25.2 0.0 all-gather.3.cloned.1.call-update
  25.2 0.0 all-reduce.2.cloned.1.call-start
  25.2 30.7 %all-gather.3.cloned.1.call-done = f32[1024,256]{1,0:T(8,128)} async-done(((f32[256,256]{1,0:T(8,128)}), f32[1024,256]{1,0:T(8,128)}) %all-gather.3.cloned.1.call-update) | async-done | bytes 1048592 | tf_op jit(solution)/shard_map/all_gather | solution.py:16
  56.0 1.3 %reduce_sum.9 = f32[256,256]{1,0:T(8,128)S(1)} reduce(f32[4,256,256]{2,1,0:T(8,128)} %bitcast.3, f32[]{:T(128)} %constant.29.clone.1), dimensions={0}, to_apply=%region_0.0 | reduce | flops 196608 | bytes 1310724 | tf_op jit(solution)/shard_map/reduce_sum | solution.py:16
  57.3 0.7 broadcast_select_fusion
  58.0 0.0 all-reduce.2.cloned.1.call-update
  58.0 31.8 %all-reduce.2.cloned.1.call-done = f32[256,256]{1,0:T(8,128)} async-done(((f32[256,256]{1,0:T(8,128)}), f32[256,256]{1,0:T(8,128)}) %all-reduce.2.cloned.1.call-update) | async-done | bytes 262160 | tf_op jit(solution)/shard_map/psum | solution.py:10
  89.8 1.7 %copy.4 = f32[256,256]{1,0:T(8,128)} copy(f32[256,256]{1,0:T(8,128)} %all-reduce.2.cloned.1.call-done) | data formatting | bytes 524288
Async XLA Ops:
  6.5 49.4 %all-gather.3.cloned.1.call-start = ((), (), s32[]{:S(2)}) async-start(), calls=%async_computation.1 | async-start | bytes 1310720 | tf_op jit(solution)/shard_map/all_gather | solution.py:16
  25.2 64.6 %all-reduce.2.cloned.1.call-start = ((), (), s32[]{:S(2)}) async-start(), calls=%async_computation | async-start | bytes 524288 | tf_op jit(solution)/shard_map/psum | solution.py:10
Sparse Core Ops, SparseCore 0:
  25.3 30.6 all-gather.2
  58.3 31.4 all-reduce.1
